TPU v7x, 128 devices: a whole 4x4x4 slice. The times are simulated.
128 devices in a mesh: row: 4 (over z_hi, core), col: 32 (over x, z_lo, y).
Axes of the slice: x: 4, y: 4, z: 4 (z_hi: 2, z_lo: 2; z = z_hi * 2 + z_lo), core: 2. Of those that a mesh axis runs over, the one named last changes fastest.
Arguments:
- right_side: float32 [131072, 128], P(('row', 'col')), may hold values from -150 to 150
- block_values: bfloat16 [64, 917504], P(None, ('row', 'col')), may hold values from -1 to 2, as said below
- block_cols: int32 [14336], P(('row', 'col')), may hold values from 0 to 511, as said below
- row_ptrs: int32 [8320], P(('row', 'col')), may hold values from 0 to 112, as said below
- precond: float32 [131072, 1024], P(('row', 'col')), may hold values from -1 to 2, as said below
Outputs:
- solution: float32 [131072, 128], P(('row', 'col'))
- residual: float32 [131072, 128], P(('row', 'col'))
Inputs may be any that keep to these rules, and one draw needn't show every extreme that they name: `row_ptrs`: in each tile t the 65 pointers from index t * (65) on never fall, start at 0 and end at 112. `block_cols`: each of the 2048 block rows of A holds 7 blocks. `block_values`: with the pattern, the blocks form a symmetric matrix A. `precond`: each 1024 x 1024 block is lower triangular with a positive diagonal.
All inputs are finite; a program needn't handle non-finite values.
Results may differ from a plain program's by a relative error of at most 0.0076.
Values may be sent and summed in bfloat16 or wider, within the bound.
A program may use at most 128 MiB of HBM per device.

v0:
```python
import jax
import jax.numpy as jnp
from jax import lax
from jax.sharding import PartitionSpec as P

ITERS = 2


def per_device(right_side, block_values, block_cols, row_ptrs, precond):
    block_size = block_values.shape[0]
    slot_count = block_cols.shape[0]
    tile_rows = row_ptrs.shape[0] - 1
    seg_rows = right_side.shape[0]
    rhs_count = right_side.shape[1]
    tile_cols = lax.axis_size("col") * (seg_rows // block_size)
    tile_blocks = block_values.reshape(block_size, slot_count, block_size)
    slot_index = jnp.arange(slot_count, dtype=jnp.int32)
    slot_rows = jnp.sum((slot_index[:, None] >= row_ptrs[None, 1:]).astype(jnp.int32), axis=1)
    solution = jnp.zeros_like(right_side)
    residual = right_side
    direction = right_side
    image_vec = right_side
    alpha_prev = jnp.ones((rhs_count,), jnp.float32)
    gamma_prev = jnp.ones((rhs_count,), jnp.float32)
    for iteration in range(ITERS):
        half_step = jnp.dot(
            precond, residual, precision=lax.Precision.HIGHEST, preferred_element_type=jnp.float32
        )
        smoothed = lax.dot_general(
            precond,
            half_step,
            (((0,), (0,)), ((), ())),
            precision=lax.Precision.HIGHEST,
            preferred_element_type=jnp.float32,
        )
        local_energy = jnp.sum(residual * smoothed, axis=0)
        gamma_now = lax.psum(local_energy, ("row", "col"))
        gathered = lax.all_gather(smoothed.astype(jnp.bfloat16), "col", axis=0, tiled=True)
        pieces = gathered.reshape(tile_cols, block_size, rhs_count)[block_cols]
        products = jnp.einsum(
            "ibj,bjk->bik", tile_blocks, pieces, preferred_element_type=jnp.float32
        )
        partial_value = jax.ops.segment_sum(
            products, slot_rows, num_segments=tile_rows, indices_are_sorted=True
        )
        applied = lax.psum_scatter(
            partial_value.reshape(tile_rows * block_size, rhs_count),
            "row",
            scatter_dimension=0,
            tiled=True,
        )
        delta_now = lax.psum(jnp.sum(smoothed * applied, axis=0), ("row", "col"))
        if iteration == 0:
            alpha_now = gamma_now / delta_now
            direction = smoothed
            image_vec = applied
        else:
            beta_now = gamma_now / gamma_prev
            alpha_now = gamma_now / (delta_now - beta_now * gamma_now / alpha_prev)
            direction = smoothed + beta_now * direction
            image_vec = applied + beta_now * image_vec
        solution = solution + alpha_now * direction
        residual = residual - alpha_now * image_vec
        gamma_prev = gamma_now
        alpha_prev = alpha_now
    return (solution, residual)


def solution(mesh):
    return jax.shard_map(
        per_device,
        mesh=mesh,
        in_specs=(
            P(("row", "col"), None),
            P(None, ("row", "col")),
            P(("row", "col")),
            P(("row", "col")),
            P(("row", "col"), None),
        ),
        out_specs=(P(("row", "col"), None), P(("row", "col"), None)),
        check_vma=False,
    )
```

profile of v0, /device:TPU:1, one launch (start us, length us, event | category | flops | bytes accessed | tf_op | source)
XLA Modules:
  0.0 653.4 jit_solution(4864520073481413777)
XLA Ops:
  7.2 5.4 fusion.5
  12.7 3.2 fusion.3
  16.0 2.3 reshape.24
  18.5 148.9 %all-gather.3.cloned.1.call-done = bf16[32768,128]{0,1:T(8,128)(2,1)} async-done(((bf16[1024,128]{0,1:T(8,128)(2,1)}), bf16[32768,128]{0,1:T(8,128)(2,1)}) %all-gather.3.cloned.1.call-update) | async-done | bytes 8388624 | tf_op jit(solution)/shard_map/all_gather | solution.py:38
  167.4 11.9 %copy.26 = bf16[32768,128]{1,0:T(8,128)(2,1)} copy(bf16[32768,128]{0,1:T(8,128)(2,1)} %all-gather.3.cloned.1.call-done) | data formatting | bytes 16777216 | tf_op jit(solution)/shard_map/all_gather | solution.py:38
  179.3 5.4 gather_fusion
  184.7 3.9 convolution_bitcast_fusion.1
  188.9 11.9 %scatter_fusion = f32[64,64,128]{2,1,0:T(8,128)S(1)} fusion(f32[64,64,128]{2,1,0:T(8,128)S(1)} %broadcast.13.clone, s32[112]{0:T(128)S(1)} %convert_reduce_fusion, f32[112,64,128]{2,1,0:T(8,128)} %convolution_bitcast_fusion.1), kind=kCustom, calls=%fused_computation.2 | custom fusion | flops 917504 | bytes 11010496 | tf_op jit(solution)/shard_map/scatter-add | solution.py:43
  200.8 1.9 copy.28
  203.9 57.5 %reduce-scatter.3.cloned.1.call-done = f32[1024,128]{0,1:T(8,128)} async-done(((f32[4096,128]{0,1:T(8,128)}), f32[1024,128]{0,1:T(8,128)}) %reduce-scatter.3.cloned.1.call-update) | async-done | bytes 524304 | tf_op jit(solution)/shard_map/reduce_scatter | solution.py:46
  261.4 1.2 multiply_reduce_fusion.2
  262.6 64.9 %all-reduce.1 = (f32[128]{0:T(128)S(1)}, f32[128]{0:T(128)S(1)}) all-reduce(f32[128]{0:T(128)S(1)} %get-tuple-element.11, f32[128]{0:T(128)S(1)} %get-tuple-element.10), channel_id=1, replica_groups=mesh['row'=4,'col'=32] {'row','col'}, use_global_device_ids=true, to_apply=%region_1.0 | all-reduce | flops 256 | bytes 2048 | tf_op jit(solution)/shard_map/psum | solution.py:37
  327.5 6.9 %fusion.2 = f32[128,1024]{1,0:T(8,128)S(1)} fusion(f32[1024,1024]{1,0:T(8,128)} %param.9, f32[1024,128]{0,1:T(8,128)S(1)} %copy.25, f32[1024,128]{0,1:T(8,128)} %reduce-scatter.3.cloned.1.call-done, f32[128]{0:T(128)S(1)} %div.12), kind=kOutput, calls=%fused_computation.22 | convolution fusion | flops 1610874880 | bytes 5767680 | tf_op jit(solution)/shard_map/dot_general | solution.py:26
  334.5 3.3 fusion.4
  337.8 145.3 %all-gather.5.cloned.1.call-done = bf16[32768,128]{0,1:T(8,128)(2,1)} async-done(((bf16[1024,128]{0,1:T(8,128)(2,1)}), bf16[32768,128]{0,1:T(8,128)(2,1)}) %all-gather.5.cloned.1.call-update) | async-done | bytes 8388624 | tf_op jit(solution)/shard_map/all_gather | solution.py:38
  483.2 11.9 %copy.30 = bf16[32768,128]{1,0:T(8,128)(2,1)} copy(bf16[32768,128]{0,1:T(8,128)(2,1)} %all-gather.5.cloned.1.call-done) | data formatting | bytes 16777216 | tf_op jit(solution)/shard_map/all_gather | solution.py:38
  495.1 5.6 gather_fusion.1
  500.7 3.9 convolution_bitcast_fusion
  504.9 11.9 %scatter_fusion.1 = f32[64,64,128]{2,1,0:T(8,128)S(1)} fusion(f32[64,64,128]{2,1,0:T(8,128)S(1)} %broadcast.13, s32[112]{0:T(128)S(1)} %convert_reduce_fusion, f32[112,64,128]{2,1,0:T(8,128)} %convolution_bitcast_fusion), kind=kCustom, calls=%fused_computation.3 | custom fusion | flops 917504 | bytes 11010496 | tf_op jit(solution)/shard_map/scatter-add | solution.py:43
  516.8 1.9 copy.32
  518.7 58.8 %reduce-scatter.5.cloned.1.call-done = f32[1024,128]{0,1:T(8,128)} async-done(((f32[4096,128]{0,1:T(8,128)}), f32[1024,128]{0,1:T(8,128)}) %reduce-scatter.5.cloned.1.call-update) | async-done | bytes 524304 | tf_op jit(solution)/shard_map/reduce_scatter | solution.py:46
  577.5 1.3 multiply_reduce_fusion
  578.7 64.7 %all-reduce = (f32[128]{0:T(128)S(1)}, f32[128]{0:T(128)S(1)}) all-reduce(f32[128]{0:T(128)S(1)} %get-tuple-element.9, f32[128]{0:T(128)S(1)} %get-tuple-element.8), channel_id=1, replica_groups=mesh['row'=4,'col'=32] {'row','col'}, use_global_device_ids=true, to_apply=%region_8.0 | all-reduce | flops 256 | bytes 2048 | tf_op jit(solution)/shard_map/psum | solution.py:37
  643.5 1.4 multiply_subtract_fusion
  (37 shorter events, 4.1 us)
Async XLA Ops:
  7.2 160.2 %all-gather.3.cloned.1.call-start = ((), (), s32[]{:S(2)}) async-start(), calls=%async_computation.2 | async-start | bytes 8650752 | tf_op jit(solution)/shard_map/all_gather | solution.py:38
  7.2 5.5 copy-start
  12.7 3.3 copy-start.7
  15.9 2.4 copy-start.8
  15.9 245.5 %reduce-scatter.3.cloned.1.call-start = ((), (), s32[]{:S(2)}) async-start(), calls=%async_computation.3 | async-start | bytes 2621440 | tf_op jit(solution)/shard_map/reduce_scatter | solution.py:46
  18.3 166.4 %copy-start.2 = (bf16[64,112,64]{2,1,0:T(8,128)(2,1)}, bf16[64,112,64]{2,1,0:T(8,128)(2,1)S(1)}, u32[]{:S(2)}) copy-start(bf16[64,112,64]{2,1,0:T(8,128)(2,1)S(1)} %reshape.24) | copy-start | bytes 2752516
  202.6 1.0 copy-start.6
  202.7 280.5 %all-gather.5.cloned.1.call-start = ((), (), s32[]{:S(2)}) async-start(), calls=%async_computation.4 | async-start | bytes 8650752 | tf_op jit(solution)/shard_map/all_gather | solution.py:38
  327.5 6.9 %copy-start.1 = (f32[1024,1024]{1,0:T(8,128)S(1)}, f32[1024,1024]{1,0:T(8,128)}, u32[]{:S(2)}) copy-start(f32[1024,1024]{1,0:T(8,128)} %param.9) | copy-start | bytes 12582916
  337.8 239.7 %reduce-scatter.5.cloned.1.call-start = ((), (), s32[]{:S(2)}) async-start(), calls=%async_computation.5 | async-start | bytes 2621440 | tf_op jit(solution)/shard_map/reduce_scatter | solution.py:46
  495.1 5.6 copy-start.3
  518.7 58.8 %copy-start.4 = (f32[1024,128]{0,1:T(8,128)S(1)}, f32[1024,128]{0,1:T(8,128)}, u32[]{:S(2)}) copy-start(f32[1024,128]{0,1:T(8,128)} %reduce-scatter.3.cloned.1.call-done) | copy-start | bytes 1572868
  518.7 58.8 %copy-start.5 = (f32[1024,128]{0,1:T(8,128)S(1)}, f32[1024,128]{0,1:T(8,128)}, u32[]{:S(2)}) copy-start(f32[1024,128]{0,1:T(8,128)} %get-tuple-element.23) | copy-start | bytes 1572868
Sparse Core Ops, SparseCore 0:
  16.0 151.3 all-gather.2
  202.8 58.5 reduce-scatter.2
  337.9 145.2 all-gather.4
  518.8 58.6 reduce-scatter.4
where the time goes:
time: 655 us; the launch traced here: 653 us
  waiting for transfers between devices  411 us (63%)
  blocking collectives  130 us (20%)
  local copies, waits for them, and re-layouts  44.6 us (7%)
  other arithmetic  27.8 us (4%)
  matrix products  26.7 us (4%)
  between operations  13.9 us (2%)
    all_gather x2, waiting for transfers between devices, per_device(): lax.all_gather(smoothed.astype(jnp.bfloat16), 'col', axis=0, tiled=True)  294 us
    psum x2, blocking collectives, per_device(): gamma_now = lax.psum(local_energy, ('row', 'col'))  130 us
    reduce_scatter x2, waiting for transfers between devices, per_device(): lax.psum_scatter(partial_value.reshape(tile_rows * block_size, rhs_count)...  116 us
    scatter-add x2, other arithmetic, per_device(): jax.ops.segment_sum(products, slot_rows, num_segments=tile_rows, indices_...  23.8 us
    all_gather x2, local copies, waits for them, and re-layouts, per_device(): lax.all_gather(smoothed.astype(jnp.bfloat16), 'col', axis=0, tiled=True)  23.8 us
  transfers between devices with their start and end apart: 4, of which 4 were waited for; matrix products, arithmetic and copies ran while one was open for 0% of the time, Pallas kernels for 0%

commit v1 on v0

--- a/solution.py
+++ b/solution.py
@@ -34,7 +34,7 @@
             preferred_element_type=jnp.float32,
         )
         local_energy = jnp.sum(residual * smoothed, axis=0)
-        gamma_now = lax.psum(local_energy, ("row", "col"))
+        gamma_now = lax.psum(lax.psum(local_energy, "col"), "row")
         gathered = lax.all_gather(smoothed.astype(jnp.bfloat16), "col", axis=0, tiled=True)
         pieces = gathered.reshape(tile_cols, block_size, rhs_count)[block_cols]
         products = jnp.einsum(

time: 655 us -> 827 us (1.26)
  blocking collectives: 130 us -> 304 us
    psum x2 -> x6, blocking collectives: 130 us -> 304 us  [the longest x4 175 us: per_device(): gamma_now = lax.psum(lax.psum(local_energy, 'col'), 'row')]
where the time goes in v1:
time: 827 us; the launch traced here: 825 us
  waiting for transfers between devices  408 us (49%)
  blocking collectives  304 us (37%)
  local copies, waits for them, and re-layouts  44.6 us (5%)
  other arithmetic  27.8 us (3%)
  matrix products  26.6 us (3%)
  between operations  13.9 us (2%)
    all_gather x2, waiting for transfers between devices, per_device(): lax.all_gather(smoothed.astype(jnp.bfloat16), 'col', axis=0, tiled=True)  292 us
    psum x4, blocking collectives, per_device(): gamma_now = lax.psum(lax.psum(local_energy, 'col'), 'row')  175 us
    psum x2, blocking collectives, per_device(): delta_now = lax.psum(jnp.sum(smoothed * applied, axis=0), ('row', 'col'))  130 us
    reduce_scatter x2, waiting for transfers between devices, per_device(): lax.psum_scatter(partial_value.reshape(tile_rows * block_size, rhs_count)...  116 us
    scatter-add x2, other arithmetic, per_device(): jax.ops.segment_sum(products, slot_rows, num_segments=tile_rows, indices_...  23.8 us
    all_gather x2, local copies, waits for them, and re-layouts, per_device(): lax.all_gather(smoothed.astype(jnp.bfloat16), 'col', axis=0, tiled=True)  23.8 us
  transfers between devices with their start and end apart: 4, of which 4 were waited for; matrix products, arithmetic and copies ran while one was open for 0% of the time, Pallas kernels for 0%

profile of v1, /device:TPU:1, one launch (start us, length us, event | category | flops | bytes accessed | tf_op | source)
XLA Modules:
  0.0 825.3 jit_solution(1791332664712663598)
XLA Ops:
  7.2 5.4 fusion.5
  12.7 3.1 fusion.3
  16.0 2.3 reshape.24
  18.4 148.9 %all-gather.3.cloned.1.call-done = bf16[32768,128]{0,1:T(8,128)(2,1)} async-done(((bf16[1024,128]{0,1:T(8,128)(2,1)}), bf16[32768,128]{0,1:T(8,128)(2,1)}) %all-gather.3.cloned.1.call-update) | async-done | bytes 8388624 | tf_op jit(solution)/shard_map/all_gather | solution.py:38
  167.3 11.9 %copy.26 = bf16[32768,128]{1,0:T(8,128)(2,1)} copy(bf16[32768,128]{0,1:T(8,128)(2,1)} %all-gather.3.cloned.1.call-done) | data formatting | bytes 16777216 | tf_op jit(solution)/shard_map/all_gather | solution.py:38
  179.2 5.4 gather_fusion
  184.7 3.9 convolution_bitcast_fusion.1
  188.8 11.9 %scatter_fusion = f32[64,64,128]{2,1,0:T(8,128)S(1)} fusion(f32[64,64,128]{2,1,0:T(8,128)S(1)} %broadcast.13.clone, s32[112]{0:T(128)S(1)} %convert_reduce_fusion, f32[112,64,128]{2,1,0:T(8,128)} %convolution_bitcast_fusion.1), kind=kCustom, calls=%fused_computation.2 | custom fusion | flops 917504 | bytes 11010496 | tf_op jit(solution)/shard_map/scatter-add | solution.py:43
  200.8 1.9 copy.28
  203.9 57.5 %reduce-scatter.3.cloned.1.call-done = f32[1024,128]{0,1:T(8,128)} async-done(((f32[4096,128]{0,1:T(8,128)}), f32[1024,128]{0,1:T(8,128)}) %reduce-scatter.3.cloned.1.call-update) | async-done | bytes 524304 | tf_op jit(solution)/shard_map/reduce_scatter | solution.py:46
  262.6 64.8 %psum.44 = f32[128]{0:T(128)S(1)} all-reduce(f32[128]{0:T(128)S(1)} %get-tuple-element.10), channel_id=1, replica_groups=mesh['row'=4,'col'=32] {'row','col'}, use_global_device_ids=true, to_apply=%region_7.0 | all-reduce | flops 128 | bytes 1024 | tf_op jit(solution)/shard_map/psum | solution.py:52
  327.4 66.0 %psum.42 = f32[128]{0:T(128)S(1)} all-reduce(f32[128]{0:T(128)S(1)} %get-tuple-element.11), channel_id=1, replica_groups=mesh['row'=4,'col'=32] {'col'}, use_global_device_ids=true, to_apply=%region_1.0 | all-reduce | flops 128 | bytes 1024 | tf_op jit(solution)/shard_map/psum | solution.py:37
  393.4 21.3 %psum.43 = f32[128]{0:T(128)S(1)} all-reduce(f32[128]{0:T(128)S(1)} %psum.42), channel_id=1, replica_groups=mesh['row'=4,'col'=32] {'row'}, use_global_device_ids=true, to_apply=%region_2.0 | all-reduce | flops 128 | bytes 1024 | tf_op jit(solution)/shard_map/psum | solution.py:37
  414.7 6.9 fusion.2
  421.7 3.3 fusion.4
  425.0 142.7 %all-gather.5.cloned.1.call-done = bf16[32768,128]{0,1:T(8,128)(2,1)} async-done(((bf16[1024,128]{0,1:T(8,128)(2,1)}), bf16[32768,128]{0,1:T(8,128)(2,1)}) %all-gather.5.cloned.1.call-update) | async-done | bytes 8388624 | tf_op jit(solution)/shard_map/all_gather | solution.py:38
  567.8 11.9 %copy.30 = bf16[32768,128]{1,0:T(8,128)(2,1)} copy(bf16[32768,128]{0,1:T(8,128)(2,1)} %all-gather.5.cloned.1.call-done) | data formatting | bytes 16777216 | tf_op jit(solution)/shard_map/all_gather | solution.py:38
  579.7 5.6 gather_fusion.1
  585.3 3.9 convolution_bitcast_fusion
  589.5 11.9 %scatter_fusion.1 = f32[64,64,128]{2,1,0:T(8,128)S(1)} fusion(f32[64,64,128]{2,1,0:T(8,128)S(1)} %broadcast.13, s32[112]{0:T(128)S(1)} %convert_reduce_fusion, f32[112,64,128]{2,1,0:T(8,128)} %convolution_bitcast_fusion), kind=kCustom, calls=%fused_computation.3 | custom fusion | flops 917504 | bytes 11010496 | tf_op jit(solution)/shard_map/scatter-add | solution.py:43
  603.3 58.8 %reduce-scatter.5.cloned.1.call-done = f32[1024,128]{0,1:T(8,128)} async-done(((f32[4096,128]{0,1:T(8,128)}), f32[1024,128]{0,1:T(8,128)}) %reduce-scatter.5.cloned.1.call-update) | async-done | bytes 524304 | tf_op jit(solution)/shard_map/reduce_scatter | solution.py:46
  663.3 64.7 %psum.47 = f32[128]{0:T(128)S(1)} all-reduce(f32[128]{0:T(128)S(1)} %get-tuple-element.8), channel_id=1, replica_groups=mesh['row'=4,'col'=32] {'row','col'}, use_global_device_ids=true, to_apply=%region_14.0 | all-reduce | flops 128 | bytes 1024 | tf_op jit(solution)/shard_map/psum | solution.py:52
  728.1 66.0 %psum.45 = f32[128]{0:T(128)S(1)} all-reduce(f32[128]{0:T(128)S(1)} %get-tuple-element.9), channel_id=1, replica_groups=mesh['row'=4,'col'=32] {'col'}, use_global_device_ids=true, to_apply=%region_9.0 | all-reduce | flops 128 | bytes 1024 | tf_op jit(solution)/shard_map/psum | solution.py:37
  794.1 21.2 %psum.46 = f32[128]{0:T(128)S(1)} all-reduce(f32[128]{0:T(128)S(1)} %psum.45), channel_id=1, replica_groups=mesh['row'=4,'col'=32] {'row'}, use_global_device_ids=true, to_apply=%region_10.0 | all-reduce | flops 128 | bytes 1024 | tf_op jit(solution)/shard_map/psum | solution.py:37
  (41 shorter events, 9.8 us)
Async XLA Ops:
  7.2 160.2 %all-gather.3.cloned.1.call-start = ((), (), s32[]{:S(2)}) async-start(), calls=%async_computation.2 | async-start | bytes 8650752 | tf_op jit(solution)/shard_map/all_gather | solution.py:38
  7.2 5.5 copy-start
  12.7 3.2 copy-start.7
  15.8 2.4 copy-start.8
  15.9 245.5 %reduce-scatter.3.cloned.1.call-start = ((), (), s32[]{:S(2)}) async-start(), calls=%async_computation.3 | async-start | bytes 2621440 | tf_op jit(solution)/shard_map/reduce_scatter | solution.py:46
  18.3 166.4 %copy-start.2 = (bf16[64,112,64]{2,1,0:T(8,128)(2,1)}, bf16[64,112,64]{2,1,0:T(8,128)(2,1)S(1)}, u32[]{:S(2)}) copy-start(bf16[64,112,64]{2,1,0:T(8,128)(2,1)S(1)} %reshape.24) | copy-start | bytes 2752516
  202.6 1.0 copy-start.6
  202.6 365.1 %all-gather.5.cloned.1.call-start = ((), (), s32[]{:S(2)}) async-start(), calls=%async_computation.4 | async-start | bytes 8650752 | tf_op jit(solution)/shard_map/all_gather | solution.py:38
  414.7 6.9 copy-start.1
  425.0 237.1 %reduce-scatter.5.cloned.1.call-start = ((), (), s32[]{:S(2)}) async-start(), calls=%async_computation.5 | async-start | bytes 2621440 | tf_op jit(solution)/shard_map/reduce_scatter | solution.py:46
  579.7 5.6 copy-start.3
  603.3 58.8 %copy-start.4 = (f32[1024,128]{0,1:T(8,128)S(1)}, f32[1024,128]{0,1:T(8,128)}, u32[]{:S(2)}) copy-start(f32[1024,128]{0,1:T(8,128)} %reduce-scatter.3.cloned.1.call-done) | copy-start | bytes 1572868
  603.3 58.8 %copy-start.5 = (f32[1024,128]{0,1:T(8,128)S(1)}, f32[1024,128]{0,1:T(8,128)}, u32[]{:S(2)}) copy-start(f32[1024,128]{0,1:T(8,128)} %get-tuple-element.19) | copy-start | bytes 1572868
Sparse Core Ops, SparseCore 0:
  16.0 151.3 all-gather.2
  202.8 58.5 reduce-scatter.2
  425.1 142.6 all-gather.4
  603.4 58.6 reduce-scatter.4
